TPU v7x, 256 devices: a whole 4x4x8 slice. The times are simulated.
256 devices in a mesh: row: 16 (over x_lo, z), col: 16 (over x_hi, y, core).
Axes of the slice: x: 4 (x_hi: 2, x_lo: 2; x = x_hi * 2 + x_lo), y: 4, z: 8, core: 2. Of those that a mesh axis runs over, the one named last changes fastest.
Arguments:
- hidden_in: bfloat16 [12288, 5120], P('row', 'col'), may hold values from -6 to 6
- modulation: bfloat16 [48, 3, 5120], P(None, None, 'col'), may hold values from -3 to 3
- w_qkv: bfloat16 [5120, 12288], P('row', 'col'), may hold values from -0.078125 to 0.078125
- w_out: bfloat16 [4096, 5120], P('row', 'col'), may hold values from -0.09375 to 0.09375
- prefix_cache: bfloat16 [16, 256, 8192], P('row', None, 'col'), may hold values from -48 to 48
- req_group: int32 [48], replicated, may hold values from 0 to 3
- req_len: int32 [48], replicated, may hold values from 1 to 672, 12288 in all
- owner: int32 [4], replicated, may hold values from 0 to 15, as said below
Outputs:
- hidden_out: bfloat16 [12288, 5120], P('row', 'col')
- suffix_keys: bfloat16 [12288, 4096], P('row', 'col')
- suffix_values: bfloat16 [12288, 4096], P('row', 'col')
Inputs may be any that keep to these rules, and one draw needn't show every extreme that they name: `owner`: the 4 slots are distinct; slot 0 and slot 16 - 1 always hold a group.
All inputs are finite; a program needn't handle non-finite values.
Results may differ from a plain program's by a relative error of at most 0.006.
Values may be sent and summed in bfloat16 or wider, within the bound.
A program may use at most 192 MiB of HBM per device.

v0:
```python
import math
import jax
import jax.numpy as jnp
from jax import lax
from jax.sharding import PartitionSpec as P

HD = 128
neg_fill = -1e30


def with_halo(block, sides, width):
    for axis, dim in sides:
        count = lax.axis_size(axis)
        forward = [(i, i + 1) for i in range(count - 1)]
        backward = [(target, source) for source, target in forward]
        low = lax.ppermute(
            lax.slice_in_dim(block, block.shape[dim] - width, None, axis=dim), axis, forward
        )
        high = lax.ppermute(lax.slice_in_dim(block, 0, width, axis=dim), axis, backward)
        block = jnp.concatenate([low, block, high], axis=dim)
    return block


def request_of(positions, req_len):
    starts = jnp.cumsum(req_len) - req_len
    inside = (starts[None, :] <= positions[:, None]).astype(jnp.int32)
    return jnp.sum(inside, axis=1) - 1


def attend(running, queries, key_block, value_block, allowed):
    largest, denominator, summed = running
    scores = jnp.einsum("thd,khd->thk", queries, key_block, preferred_element_type=jnp.float32)
    scores = scores * (1.0 / math.sqrt(queries.shape[-1]))
    widened = allowed[:, None, :]
    scores = jnp.where(widened, scores, neg_fill)
    new_largest = jnp.maximum(largest, jnp.max(scores, axis=2))
    weights = jnp.where(widened, jnp.exp(scores - new_largest[:, :, None]), 0.0)
    rescale = jnp.exp(largest - new_largest)
    denominator = denominator * rescale + jnp.sum(weights, axis=2)
    summed = summed * rescale[:, :, None] + jnp.einsum(
        "thk,khd->thd",
        weights.astype(jnp.bfloat16),
        value_block,
        preferred_element_type=jnp.float32,
    )
    return (new_largest, denominator, summed)


def shards(hidden_in, modulation, w_qkv, w_out, prefix_cache, req_group, req_len, owner):
    token_rows = hidden_in.shape[0]
    full_hidden, full_modulation = (
        lax.all_gather(hidden_in, "col", axis=1, tiled=True),
        lax.all_gather(modulation, "col", axis=2, tiled=True),
    )
    full_width = full_hidden.shape[1]
    requests = req_len.shape[0]
    row_index = lax.axis_index("row")
    positions = row_index * token_rows + jnp.arange(token_rows, dtype=jnp.int32)
    request_id = request_of(positions, req_len)
    matches = request_id[:, None] == jnp.arange(requests, dtype=jnp.int32)[None, :]
    onehot = matches.astype(jnp.bfloat16)
    per_token = jnp.dot(
        onehot,
        full_modulation.reshape(requests, 3 * full_width),
        preferred_element_type=jnp.float32,
    )
    shift_rows = per_token[:, :full_width]
    scale_rows = per_token[:, full_width : 2 * full_width]
    gate_rows = jnp.dot(onehot, modulation[:, 2, :], preferred_element_type=jnp.float32)
    token_group = jnp.sum(jnp.where(matches, req_group[None, :], 0), axis=1)
    hidden_f = full_hidden.astype(jnp.float32)
    average = jnp.mean(hidden_f, axis=1, keepdims=True)
    centred = hidden_f - average
    variance = jnp.mean(centred * centred, axis=1, keepdims=True)
    modulated = (centred * lax.rsqrt(variance + 1e-06) * (1.0 + scale_rows) + shift_rows).astype(
        jnp.bfloat16
    )
    projected_qkv = jnp.dot(
        modulated,
        lax.all_gather(w_qkv, "row", axis=0, tiled=True),
        preferred_element_type=jnp.float32,
    )
    local_heads = w_qkv.shape[1] // (3 * HD)
    projected_qkv = projected_qkv.astype(jnp.bfloat16).reshape(token_rows, local_heads, 3, HD)
    queries = projected_qkv[:, :, 0]
    new_keys = projected_qkv[:, :, 1]
    new_values = projected_qkv[:, :, 2]
    key_value = projected_qkv[:, :, 1:].reshape(token_rows, local_heads * 2 * HD)
    surrounded = with_halo(key_value, (("row", 0),), token_rows)
    running = (
        jnp.full((token_rows, local_heads), neg_fill, jnp.float32),
        jnp.zeros((token_rows, local_heads), jnp.float32),
        jnp.zeros((token_rows, local_heads, HD), jnp.float32),
    )

    def slot_attend(carried, slot_data, group_number):
        present = token_group == group_number
        arranged = slot_data.reshape(slot_data.shape[0], local_heads, 2, HD)
        allowed = jnp.broadcast_to(present[:, None], (token_rows, slot_data.shape[0]))
        return attend(carried, queries, arranged[:, :, 0], arranged[:, :, 1], allowed)

    group_numbers = jnp.arange(owner.shape[0], dtype=jnp.int32)
    slot_block = lax.all_gather(prefix_cache, "row", axis=0, tiled=True)

    def one_slot(offset, current):
        group_number = jnp.sum(jnp.where(owner == offset, group_numbers + 1, 0)) - 1
        slot_data = lax.dynamic_index_in_dim(slot_block, offset, 0, keepdims=False)
        return slot_attend(current, slot_data, group_number)

    running = lax.fori_loop(0, slot_block.shape[0], one_slot, running)
    near_pairs = surrounded.reshape(3 * token_rows, local_heads, 2, HD)
    key_pos = (row_index - 1) * token_rows + jnp.arange(3 * token_rows, dtype=jnp.int32)
    key_req = request_of(key_pos, req_len)
    inside_range = key_pos < jnp.sum(req_len)
    near_mask = (key_req[None, :] == request_id[:, None]) & inside_range[None, :]
    running = attend(running, queries, near_pairs[:, :, 0], near_pairs[:, :, 1], near_mask)
    largest, denominator, summed = running
    attended = (
        (summed / denominator[:, :, None])
        .astype(jnp.bfloat16)
        .reshape(token_rows, local_heads * HD)
    )
    out_weight = lax.all_gather(w_out, "row", axis=0, tiled=True)
    projected = jnp.dot(
        lax.all_gather(attended, "col", axis=1, tiled=True),
        out_weight,
        preferred_element_type=jnp.float32,
    )
    hidden_out = (hidden_in.astype(jnp.float32) + gate_rows * projected).astype(jnp.bfloat16)
    return (
        hidden_out,
        new_keys.reshape(token_rows, local_heads * HD),
        new_values.reshape(token_rows, local_heads * HD),
    )


def solution(mesh):
    return jax.shard_map(
        shards,
        mesh=mesh,
        in_specs=(
            P("row", "col"),
            P(None, None, "col"),
            P("row", "col"),
            P("row", "col"),
            P("row", None, "col"),
            P(),
            P(),
            P(),
        ),
        out_specs=(P("row", "col"), P("row", "col"), P("row", "col")),
        check_vma=False,
    )
```

profile of v0, /device:TPU:1, one launch (start us, length us, event | category | flops | bytes accessed | tf_op | source)
XLA Modules:
  0.0 497.8 jit_solution(4544151833377507003)
XLA Ops:
  7.2 1.8 copy.59
  12.7 1.3 fusion.60
  15.7 2.9 compare_and_fusion
  18.6 61.9 %all-gather.11.cloned.1.call-done = bf16[48,3,5120]{0,1,2:T(4,128)(2,1)} async-done(((bf16[48,3,320]{0,1,2:T(4,128)(2,1)}), bf16[48,3,5120]{0,1,2:T(4,128)(2,1)}) %all-gather.11.cloned.1.call-update) | async-done | bytes 1474576 | tf_op jit(solution)/shard_map/all_gather | solution.py:53
  80.4 7.7 %copy.60 = bf16[48,3,5120]{2,1,0:T(4,128)(2,1)S(1)} copy(bf16[48,3,5120]{0,1,2:T(4,128)(2,1)} %all-gather.11.cloned.1.call-done) | data formatting | bytes 2949120 | tf_op jit(solution)/shard_map/all_gather | solution.py:53
  88.8 18.8 %fusion.48 = f32[768,15360]{1,0:T(8,128)} fusion(bf16[48,15360]{1,0:T(8,128)(2,1)S(1)} %bitcast.111, s32[768]{0:T(1024)S(1)} %broadcast_add_fusion.1), kind=kOutput, calls=%fused_computation.61 | convolution fusion | flops 1132498944 | bytes 48663552 | tf_op jit(solution)/shard_map/dot_general | solution.py:62
  107.5 49.4 %all-gather.9.cloned.1.call-done = bf16[768,5120]{0,1:T(8,128)(2,1)} async-done(((bf16[768,320]{0,1:T(8,128)(2,1)}), bf16[768,5120]{0,1:T(8,128)(2,1)}) %all-gather.9.cloned.1.call-update) | async-done | bytes 7864336 | tf_op jit(solution)/shard_map/all_gather | solution.py:52
  156.9 10.7 %copy.58 = bf16[768,5120]{1,0:T(8,128)(2,1)} copy(bf16[768,5120]{0,1:T(8,128)(2,1)} %all-gather.9.cloned.1.call-done) | data formatting | bytes 15728640 | tf_op jit(solution)/shard_map/all_gather | solution.py:52
  167.6 4.5 convert_reduce_fusion
  172.1 1.0 copy-done
  173.1 2.2 fusion.17
  175.3 76.6 %all-gather.13.cloned.1.call-done = bf16[5120,768]{1,0:T(8,128)(2,1)} async-done(((bf16[320,768]{1,0:T(8,128)(2,1)}), bf16[5120,768]{1,0:T(8,128)(2,1)}) %all-gather.13.cloned.1.call-update) | async-done | bytes 7864336 | tf_op jit(solution)/shard_map/all_gather | solution.py:80
  251.9 21.3 %fusion.29 = bf16[768,768]{0,1:T(8,128)(2,1)S(1)} fusion(bf16[5120,768]{1,0:T(8,128)(2,1)} %all-gather.13.cloned.1.call-done, bf16[768,5120]{1,0:T(8,128)(2,1)} %copy.58, f32[768,15360]{1,0:T(8,128)} %fusion.48, f32[768]{0:T(1024)S(1)} %add_rsqrt_fusion, f32[768]{0:T(1024)S(1)} %broadcast_multiply_fusion), kind=kOutput, calls=%fused_computation.46 | convolution fusion | flops 6067912704 | bytes 48371712 | tf_op jit(solution)/shard_map/dot_general | solution.py:78
  273.2 1.0 slice.63
  274.3 2.2 collective-permute-start
  276.4 1.5 collective-permute-start.1
  279.1 51.5 %all-gather.7.cloned.1.call-done = bf16[16,256,512]{2,1,0:T(8,128)(2,1)} async-done(((bf16[1,256,512]{2,1,0:T(8,128)(2,1)}), bf16[16,256,512]{2,1,0:T(8,128)(2,1)}) %all-gather.7.cloned.1.call-update) | async-done | bytes 4194320 | tf_op jit(solution)/shard_map/all_gather | solution.py:103
  330.6 58.0 %while.20 = (s32[]{:T(128)}, f32[768,2]{0,1:T(2,128)S(1)}, f32[768,2]{0,1:T(2,128)S(1)}, f32[768,2,128]{0,2,1:T(8,128)S(1)}, s32[4]{0:T(128)S(1)}, /*index=5*/s3...) while((s32[]{:T(128)}, f32[768,2]{0,1:T(2,128)S(1)}, ...), condition=%wide.region_9.10_spmd.clone, body=%wide.region_5.9_spmd.clone.sunk | while | flops 205463824 | bytes 8100517 | solution.py:110
  368.1 1.0 constant_dynamic-slice_fusion.2
  371.7 1.0 constant_dynamic-slice_fusion.2
  375.3 1.0 constant_dynamic-slice_fusion.2
  379.0 1.0 constant_dynamic-slice_fusion.2
  388.6 1.6 copy.80
  390.3 2.3 copy.65
  392.6 2.3 copy.66
  394.9 1.5 pad_maximum_fusion
  396.4 4.2 fusion.21
  400.7 4.0 fusion.22
  404.7 5.7 %fusion.44 = bf16[768,2,128]{0,2,1:T(8,128)(2,1)} fusion(f32[2,2304,768]{2,1,0:T(8,128)S(1)} %get-tuple-element.301, f32[768,2]{0,1:T(2,128)S(1)} %max.13, pred[768,2304]{0,1:T(8,128)(4,1)S(1)} %copy-done.1, bf16[2304,2,2,128]{3,0,1,2:T(8,128)(2,1)} %copy-done.3, f32[768,2,128]{0,2,1:T(8,128)S(1)} %get-tuple-element.225, ...), kind=kOutput, calls=%fused_computation.56 | convolution fusion | flops 924450816 | bytes 18302976 | tf_op jit(solution)/shard_map/thk,khd->thd/dot_general | solution.py:40
  410.5 1.1 fusion.49
  413.4 71.0 %all-gather.15.cloned.1.call-done = bf16[768,4096]{0,1:T(8,128)(2,1)} async-done(((bf16[768,256]{0,1:T(8,128)(2,1)}), bf16[768,4096]{0,1:T(8,128)(2,1)}) %all-gather.15.cloned.1.call-update) | async-done | bytes 6291472 | tf_op jit(solution)/shard_map/all_gather | solution.py:125
  484.4 6.6 %fusion.36 = bf16[768,320]{0,1:T(8,128)(2,1)} fusion(f32[768,320]{0,1:T(8,128)S(1)} %fusion.49, bf16[4096,320]{0,1:T(8,128)(2,1)} %all-gather.17.cloned.1.call-done, bf16[768,4096]{0,1:T(8,128)(2,1)} %all-gather.15.cloned.1.call-done, bf16[768,320]{0,1:T(8,128)(2,1)} %param.10), kind=kOutput, calls=%fused_computation.50 | convolution fusion | flops 2014248960 | bytes 10878976 | tf_op jit(solution)/shard_map/dot_general | solution.py:124
  (207 shorter events, 52.7 us)
Async XLA Ops:
  7.2 73.3 %all-gather.11.cloned.1.call-start = ((), (), s32[]{:S(2)}) async-start(), calls=%async_computation.2 | async-start | bytes 5570560 | tf_op jit(solution)/shard_map/all_gather | solution.py:53
  9.1 147.9 %all-gather.9.cloned.1.call-start = ((), (), s32[]{:S(2)}) async-start(), calls=%async_computation.1 | async-start | bytes 8355840 | tf_op jit(solution)/shard_map/all_gather | solution.py:52
  9.8 242.1 %all-gather.13.cloned.1.call-start = ((), (), s32[]{:S(2)}) async-start(), calls=%async_computation.3 | async-start | bytes 8355840 | tf_op jit(solution)/shard_map/all_gather | solution.py:80
  10.5 320.1 %all-gather.7.cloned.1.call-start = ((), (), s32[]{:S(2)}) async-start(), calls=%async_computation | async-start | bytes 4456448 | tf_op jit(solution)/shard_map/all_gather | solution.py:103
  11.1 402.3 %all-gather.17.cloned.1.call-start = ((), (), s32[]{:S(2)}) async-start(), calls=%async_computation.5 | async-start | bytes 2785280 | tf_op jit(solution)/shard_map/all_gather | solution.py:123
  11.7 472.7 %all-gather.15.cloned.1.call-start = ((), (), s32[]{:S(2)}) async-start(), calls=%async_computation.4 | async-start | bytes 6684672 | tf_op jit(solution)/shard_map/all_gather | solution.py:125
  167.6 5.5 %copy-start = (bf16[768,5120]{1,0:T(8,128)(2,1)S(1)}, bf16[768,5120]{1,0:T(8,128)(2,1)}, u32[]{:S(2)}) copy-start(bf16[768,5120]{1,0:T(8,128)(2,1)} %copy.58) | copy-start | bytes 23592964
  175.3 155.3 %copy-start.6 = (s32[4]{0:T(128)S(1)}, s32[4]{0:T(128)}, u32[]{:S(2)}) copy-start(s32[4]{0:T(128)} %param.17) | copy-start | bytes 52
  273.2 5.6 %copy-start.2 = (bf16[768,768]{0,1:T(8,128)(2,1)}, bf16[768,768]{0,1:T(8,128)(2,1)S(1)}, u32[]{:S(2)}) copy-start(bf16[768,768]{0,1:T(8,128)(2,1)S(1)} %fusion.29) | copy-start | bytes 3538948
  274.3 116.0 %collective-permute-start = (bf16[768,512]{0,1:T(8,128)(2,1)}, bf16[768,512]{0,1:T(8,128)(2,1)}, u32[]{:S(2)}, u32[]{:S(2)}) collective-permute-start(bf16[768,512]{0,1:T(8,128)(2,1)} %bitcast.4), channel_id=1, source_target_pairs={{0,16},{16,32},{32,48},{48,64},{64,80},{80,96},{96,112},{112,128},... | collective-permute-start | bytes 2359304 | tf_op jit(solution)/shard_map/ppermute | solution.py:16
  276.4 116.2 %collective-permute-start.1 = (bf16[768,512]{0,1:T(8,128)(2,1)}, bf16[768,512]{0,1:T(8,128)(2,1)}, u32[]{:S(2)}, u32[]{:S(2)}) collective-permute-start(bf16[768,512]{0,1:T(8,128)(2,1)} %bitcast.4), channel_id=1, source_target_pairs={{16,0},{32,16},{48,32},{64,48},{80,64},{96,80},{112,96},{128,112},... | collective-permute-start | bytes 2359304 | tf_op jit(solution)/shard_map/ppermute | solution.py:19
  388.6 7.8 %copy-start.1 = (pred[768,2304]{0,1:T(8,128)(4,1)S(1)}, pred[768,2304]{0,1:T(8,128)(4,1)}, u32[]{:S(2)}) copy-start(pred[768,2304]{0,1:T(8,128)(4,1)} %compare_and_fusion) | copy-start | bytes 5308420
  396.4 4.2 copy-start.3
  404.7 6.9 %copy-start.5 = (bf16[768,2,1,128]{0,3,2,1:T(8,128)(2,1)S(1)}, bf16[768,2,1,128]{0,3,2,1:T(8,128)(2,1)}, u32[]{:S(2)}) copy-start(bf16[768,2,1,128]{0,3,2,1:T(8,128)(2,1)} %get-tuple-element.297) | copy-start | bytes 1179652
  404.7 7.8 %copy-start.4 = (bf16[768,2,1,128]{0,3,2,1:T(8,128)(2,1)S(1)}, bf16[768,2,1,128]{0,3,2,1:T(8,128)(2,1)}, u32[]{:S(2)}) copy-start(bf16[768,2,1,128]{0,3,2,1:T(8,128)(2,1)} %get-tuple-element.295) | copy-start | bytes 1179652
Sparse Core Ops, SparseCore 0:
  11.3 69.0 all-gather.10
  83.2 73.6 all-gather.8
  158.7 93.1 all-gather.12
  253.6 77.0 all-gather.6
  332.2 69.7 all-gather.16
  410.6 73.7 all-gather.14
where the time goes:
time: 499 us; the launch traced here: 498 us
  waiting for transfers between devices  313 us (63%)
  matrix products  72.6 us (15%)
  local copies, waits for them, and re-layouts  50.6 us (10%)
  other arithmetic  33.2 us (7%)
  between operations  14.4 us (3%)
  loops' own time  10.3 us (2%)
    all_gather x1, waiting for transfers between devices, shards(): lax.all_gather(w_qkv, 'row', axis=0, tiled=True)  76.6 us
    all_gather x1, waiting for transfers between devices, shards(): lax.all_gather(attended, 'col', axis=1, tiled=True)  71 us
    all_gather x1, waiting for transfers between devices, shards(): lax.all_gather(modulation, 'col', axis=2, tiled=True)  61.9 us
    all_gather x1, waiting for transfers between devices, shards(): slot_block = lax.all_gather(prefix_cache, 'row', axis=0, tiled=True)  51.5 us
    all_gather x1, waiting for transfers between devices, shards(): lax.all_gather(hidden_in, 'col', axis=1, tiled=True)  49.4 us
    dot_general x1, matrix products, shards(): jnp.dot(modulated, lax.all_gather(w_qkv, 'row', axis=0, tiled=True), pref...  21.3 us
    dot_general x1, matrix products, shards(): jnp.dot(onehot, full_modulation.reshape(requests, 3 * full_width), prefer...  18.8 us
    dynamic_slice x32, local copies, waits for them, and re-layouts, one_slot(): slot_data = lax.dynamic_index_in_dim(slot_block, offset, 0, keepdims=False)  17.7 us
  transfers between devices with their start and end apart: 8, of which 5 were waited for; matrix products, arithmetic and copies ran while one was open for 30% of the time, Pallas kernels for 0%

commit v1 on v0

--- a/solution.py
+++ b/solution.py
@@ -1,11 +1,24 @@
+import functools
 import math
 import jax
 import jax.numpy as jnp
 from jax import lax
 from jax.sharding import PartitionSpec as P
+from jax.lax import all_to_all, axis_size
 
 HD = 128
 neg_fill = -1e30
+
+
+def reach_the_corner(chunk, ndim_at):
+    gallery = []
+    for _ in range(axis_size("row")):
+        gallery.append(chunk)
+    y1 = all_to_all(jnp.stack(gallery), "row", 0, 0)
+    return jnp.concatenate(y1, ndim_at)
+
+
+read_lots_all = functools.partial(reach_the_corner, ndim_at=0)
 
 
 def with_halo(block, sides, width):
@@ -75,11 +88,7 @@
     modulated = (centred * lax.rsqrt(variance + 1e-06) * (1.0 + scale_rows) + shift_rows).astype(
         jnp.bfloat16
     )
-    projected_qkv = jnp.dot(
-        modulated,
-        lax.all_gather(w_qkv, "row", axis=0, tiled=True),
-        preferred_element_type=jnp.float32,
-    )
+    projected_qkv = jnp.dot(modulated, read_lots_all(w_qkv), preferred_element_type=jnp.float32)
     local_heads = w_qkv.shape[1] // (3 * HD)
     projected_qkv = projected_qkv.astype(jnp.bfloat16).reshape(token_rows, local_heads, 3, HD)
     queries = projected_qkv[:, :, 0]

time: 499 us -> 476 us (0.954)
  waiting for transfers between devices: 313 us -> 271 us
  starting transfers between devices: 3.87 us -> 19.7 us
    all_gather x1 -> x0, waiting for transfers between devices: 76.6 us -> none  [shards(): lax.all_gather(w_qkv, 'row', axis=0, tiled=True)]
    all_gather x1, waiting for transfers between devices: 49.4 us -> 98 us  [shards(): lax.all_gather(hidden_in, 'col', axis=1, tiled=True)]
    all_gather x1, waiting for transfers between devices: 51.5 us -> 24.7 us  [shards(): slot_block = lax.all_gather(prefix_cache, 'row', axis=0, tiled=True)]
    all_gather x1, waiting for transfers between devices: 61.9 us -> 73.6 us  [shards(): lax.all_gather(modulation, 'col', axis=2, tiled=True)]
    all_to_all x0 -> x1, starting transfers between devices: none -> 10.2 us  [reach_the_corner(): y1 = all_to_all(jnp.stack(gallery), 'row', 0, 0)]
    ppermute x1, starting transfers between devices: 2.18 us -> 7.98 us  [with_halo(): lax.ppermute(lax.slice_in_dim(block, block.shape[dim] - width, None, axis...]
  transfers between devices with their start and end apart: 8 -> 8, of which waited for: 5 -> 4; matrix products, arithmetic and copies ran while one was open for 30% -> 32% of each run, Pallas kernels for 0% -> 0%
where the time goes in v1:
time: 476 us; the launch traced here: 475 us
  waiting for transfers between devices  271 us (57%)
  matrix products  72.6 us (15%)
  local copies, waits for them, and re-layouts  54.8 us (12%)
  other arithmetic  31.9 us (7%)
  starting transfers between devices  19.7 us (4%)
  between operations  14.1 us (3%)
  loops' own time  10.3 us (2%)
    all_gather x1, waiting for transfers between devices, shards(): lax.all_gather(hidden_in, 'col', axis=1, tiled=True)  98 us
    all_gather x1, waiting for transfers between devices, shards(): lax.all_gather(modulation, 'col', axis=2, tiled=True)  73.6 us
    all_gather x1, waiting for transfers between devices, shards(): lax.all_gather(attended, 'col', axis=1, tiled=True)  73 us
    all_gather x1, waiting for transfers between devices, shards(): slot_block = lax.all_gather(prefix_cache, 'row', axis=0, tiled=True)  24.7 us
    dot_general x1, matrix products, shards(): jnp.dot(modulated, read_lots_all(w_qkv), preferred_element_type=jnp.float32)  21.6 us
    dot_general x1, matrix products, shards(): jnp.dot(onehot, full_modulation.reshape(requests, 3 * full_width), prefer...  18.5 us
    dynamic_slice x32, local copies, waits for them, and re-layouts, one_slot(): slot_data = lax.dynamic_index_in_dim(slot_block, offset, 0, keepdims=False)  17.7 us
    dot_general x17, matrix products, attend(): jnp.einsum('thk,khd->thd', weights.astype(jnp.bfloat16), value_block, pre...  13.7 us
  transfers between devices with their start and end apart: 8, of which 4 were waited for; matrix products, arithmetic and copies ran while one was open for 32% of the time, Pallas kernels for 0%

profile of v1, /device:TPU:1, one launch (start us, length us, event | category | flops | bytes accessed | tf_op | source)
XLA Modules:
  0.0 474.7 jit_solution(5408674610705391747)
XLA Ops:
  7.2 1.8 copy.59
  9.8 4.9 %stack.2 = bf16[16,320,768]{2,1,0:T(8,128)(2,1)} broadcast(bf16[320,768]{1,0:T(8,128)(2,1)} %param.12), dimensions={1,2} | broadcast | bytes 8355840 | tf_op jit(solution)/shard_map/stack | solution.py:17
  14.7 10.2 %all-to-all-start = ((bf16[16,320,768]{2,1,0:T(8,128)(2,1)}), bf16[16,320,768]{2,1,0:T(8,128)(2,1)}, u32[]{:S(2)}, u32[]{:S(2)}) async-start(bf16[16,320,768]{2,1,0:T(8,128)(2,1)} %stack.2), calls=%async_computation | async-start | bytes 15728640 | tf_op jit(solution)/shard_map/all_to_all | solution.py:17
  28.3 2.8 compare_and_fusion
  31.1 73.6 %all-gather.10.cloned.1.call-done = bf16[48,3,5120]{0,1,2:T(4,128)(2,1)} async-done(((bf16[48,3,320]{0,1,2:T(4,128)(2,1)}), bf16[48,3,5120]{0,1,2:T(4,128)(2,1)}) %all-gather.10.cloned.1.call-update) | async-done | bytes 1474576 | tf_op jit(solution)/shard_map/all_gather | solution.py:66
  104.7 7.7 %copy.60 = bf16[48,3,5120]{2,1,0:T(4,128)(2,1)S(1)} copy(bf16[48,3,5120]{0,1,2:T(4,128)(2,1)} %all-gather.10.cloned.1.call-done) | data formatting | bytes 2949120 | tf_op jit(solution)/shard_map/all_gather | solution.py:66
  113.0 18.5 %fusion.48 = f32[768,15360]{1,0:T(8,128)} fusion(bf16[48,15360]{1,0:T(8,128)(2,1)S(1)} %bitcast.112, s32[768]{0:T(1024)S(1)} %broadcast_add_fusion.1), kind=kOutput, calls=%fused_computation.61 | convolution fusion | flops 1132498944 | bytes 48663552 | tf_op jit(solution)/shard_map/dot_general | solution.py:75
  131.5 98.0 %all-gather.8.cloned.1.call-done = bf16[768,5120]{0,1:T(8,128)(2,1)} async-done(((bf16[768,320]{0,1:T(8,128)(2,1)}), bf16[768,5120]{0,1:T(8,128)(2,1)}) %all-gather.8.cloned.1.call-update) | async-done | bytes 7864336 | tf_op jit(solution)/shard_map/all_gather | solution.py:65
  229.6 10.7 %copy.58 = bf16[768,5120]{1,0:T(8,128)(2,1)} copy(bf16[768,5120]{0,1:T(8,128)(2,1)} %all-gather.8.cloned.1.call-done) | data formatting | bytes 15728640 | tf_op jit(solution)/shard_map/all_gather | solution.py:65
  240.3 4.5 convert_reduce_fusion
  244.8 1.0 copy-done
  245.8 2.2 fusion.17
  248.0 21.6 %fusion.29 = bf16[768,768]{0,1:T(8,128)(2,1)S(1)} fusion(bf16[5120,768]{1,0:T(8,128)(2,1)} %bitcast.2, bf16[768,5120]{1,0:T(8,128)(2,1)} %copy.58, f32[768,15360]{1,0:T(8,128)} %fusion.48, f32[768]{0:T(1024)S(1)} %add_rsqrt_fusion, f32[768]{0:T(1024)S(1)} %broadcast_multiply_fusion), kind=kOutput, calls=%fused_computation.46 | convolution fusion | flops 6067912704 | bytes 48371712 | tf_op jit(solution)/shard_map/dot_general | solution.py:91
  269.6 1.0 slice.63
  270.6 1.3 collective-permute-start.1
  271.9 8.0 %collective-permute-start = (bf16[768,512]{0,1:T(8,128)(2,1)}, bf16[768,512]{0,1:T(8,128)(2,1)}, u32[]{:S(2)}, u32[]{:S(2)}) collective-permute-start(bf16[768,512]{0,1:T(8,128)(2,1)} %bitcast.5), channel_id=1, source_target_pairs={{0,16},{16,32},{32,48},{48,64},{64,80},{80,96},{96,112},{112,128},... | collective-permute-start | bytes 2359304 | tf_op jit(solution)/shard_map/ppermute | solution.py:29
  281.0 24.7 %all-gather.6.cloned.1.call-done = bf16[16,256,512]{2,1,0:T(8,128)(2,1)} async-done(((bf16[1,256,512]{2,1,0:T(8,128)(2,1)}), bf16[16,256,512]{2,1,0:T(8,128)(2,1)}) %all-gather.6.cloned.1.call-update) | async-done | bytes 4194320 | tf_op jit(solution)/shard_map/all_gather | solution.py:112
  305.8 58.0 %while.20 = (s32[]{:T(128)}, f32[768,2]{0,1:T(2,128)S(1)}, f32[768,2]{0,1:T(2,128)S(1)}, f32[768,2,128]{0,2,1:T(8,128)S(1)}, s32[4]{0:T(128)S(1)}, /*index=5*/s3...) while((s32[]{:T(128)}, f32[768,2]{0,1:T(2,128)S(1)}, ...), condition=%wide.region_9.10_spmd.clone, body=%wide.region_5.9_spmd.clone.sunk | while | flops 205463824 | bytes 8100525 | solution.py:119
  342.0 1.0 constant_dynamic-slice_fusion.2
  345.6 1.0 constant_dynamic-slice_fusion.2
  349.2 1.0 constant_dynamic-slice_fusion.2
  352.9 1.0 constant_dynamic-slice_fusion.2
  363.8 1.6 copy.80
  365.4 2.3 copy.66
  367.7 2.3 copy.65
  370.0 1.6 pad_maximum_fusion
  371.6 4.2 fusion.21
  375.8 4.0 fusion.22
  379.9 5.7 %fusion.44 = bf16[768,2,128]{0,2,1:T(8,128)(2,1)} fusion(f32[2,2304,768]{2,1,0:T(8,128)S(1)} %get-tuple-element.301, f32[768,2]{0,1:T(2,128)S(1)} %max.13, pred[768,2304]{0,1:T(8,128)(4,1)S(1)} %copy-done.1, bf16[2304,2,2,128]{3,0,1,2:T(8,128)(2,1)} %copy-done.3, f32[768,2,128]{0,2,1:T(8,128)S(1)} %get-tuple-element.225, ...), kind=kOutput, calls=%fused_computation.56 | convolution fusion | flops 924450816 | bytes 18302976 | tf_op jit(solution)/shard_map/thk,khd->thd/dot_general | solution.py:53
  385.6 1.1 fusion.49
  388.6 73.0 %all-gather.12.cloned.1.call-done = bf16[768,4096]{0,1:T(8,128)(2,1)} async-done(((bf16[768,256]{0,1:T(8,128)(2,1)}), bf16[768,4096]{0,1:T(8,128)(2,1)}) %all-gather.12.cloned.1.call-update) | async-done | bytes 6291472 | tf_op jit(solution)/shard_map/all_gather | solution.py:134
  461.6 6.6 %fusion.36 = bf16[768,320]{0,1:T(8,128)(2,1)} fusion(f32[768,320]{0,1:T(8,128)S(1)} %fusion.49, bf16[4096,320]{0,1:T(8,128)(2,1)} %all-gather.14.cloned.1.call-done, bf16[768,4096]{0,1:T(8,128)(2,1)} %all-gather.12.cloned.1.call-done, bf16[768,320]{0,1:T(8,128)(2,1)} %param.10), kind=kOutput, calls=%fused_computation.50 | convolution fusion | flops 2014248960 | bytes 10878976 | tf_op jit(solution)/shard_map/dot_general | solution.py:133
  (211 shorter events, 51.5 us)
Async XLA Ops:
  7.2 97.5 %all-gather.10.cloned.1.call-start = ((), (), s32[]{:S(2)}) async-start(), calls=%async_computation.3 | async-start | bytes 5570560 | tf_op jit(solution)/shard_map/all_gather | solution.py:66
  9.1 220.5 %all-gather.8.cloned.1.call-start = ((), (), s32[]{:S(2)}) async-start(), calls=%async_computation.2 | async-start | bytes 8355840 | tf_op jit(solution)/shard_map/all_gather | solution.py:65
  14.7 11.6 %copy-start.6 = (s32[48]{0:T(128)S(1)}, s32[48]{0:T(128)}, u32[]{:S(2)}) copy-start(s32[48]{0:T(128)} %param.16) | copy-start | bytes 580
  14.7 13.4 %copy-start.7 = (s32[48]{0:T(128)S(1)}, s32[48]{0:T(128)}, u32[]{:S(2)}) copy-start(s32[48]{0:T(128)} %param.15) | copy-start | bytes 580
  14.7 233.3 %all-to-all-start = ((bf16[16,320,768]{2,1,0:T(8,128)(2,1)}), bf16[16,320,768]{2,1,0:T(8,128)(2,1)}, u32[]{:S(2)}, u32[]{:S(2)}) async-start(bf16[16,320,768]{2,1,0:T(8,128)(2,1)} %stack.2), calls=%async_computation | async-start | bytes 15728640 | tf_op jit(solution)/shard_map/all_to_all | solution.py:17
  24.9 280.9 %all-gather.6.cloned.1.call-start = ((), (), s32[]{:S(2)}) async-start(), calls=%async_computation.1 | async-start | bytes 4456448 | tf_op jit(solution)/shard_map/all_gather | solution.py:112
  25.7 362.9 %all-gather.14.cloned.1.call-start = ((), (), s32[]{:S(2)}) async-start(), calls=%async_computation.5 | async-start | bytes 2785280 | tf_op jit(solution)/shard_map/all_gather | solution.py:132
  26.2 435.4 %all-gather.12.cloned.1.call-start = ((), (), s32[]{:S(2)}) async-start(), calls=%async_computation.4 | async-start | bytes 6684672 | tf_op jit(solution)/shard_map/all_gather | solution.py:134
  240.3 5.5 %copy-start = (bf16[768,5120]{1,0:T(8,128)(2,1)S(1)}, bf16[768,5120]{1,0:T(8,128)(2,1)}, u32[]{:S(2)}) copy-start(bf16[768,5120]{1,0:T(8,128)(2,1)} %copy.58) | copy-start | bytes 23592964
  247.9 57.8 %copy-start.8 = (s32[4]{0:T(128)S(1)}, s32[4]{0:T(128)}, u32[]{:S(2)}) copy-start(s32[4]{0:T(128)} %param.17) | copy-start | bytes 52
  269.6 11.3 %copy-start.2 = (bf16[768,768]{0,1:T(8,128)(2,1)}, bf16[768,768]{0,1:T(8,128)(2,1)S(1)}, u32[]{:S(2)}) copy-start(bf16[768,768]{0,1:T(8,128)(2,1)S(1)} %fusion.29) | copy-start | bytes 3538948
  270.6 94.8 %collective-permute-start.1 = (bf16[768,512]{0,1:T(8,128)(2,1)}, bf16[768,512]{0,1:T(8,128)(2,1)}, u32[]{:S(2)}, u32[]{:S(2)}) collective-permute-start(bf16[768,512]{0,1:T(8,128)(2,1)} %bitcast.5), channel_id=1, source_target_pairs={{16,0},{32,16},{48,32},{64,48},{80,64},{96,80},{112,96},{128,112},... | collective-permute-start | bytes 2359304 | tf_op jit(solution)/shard_map/ppermute | solution.py:32
  271.9 95.8 %collective-permute-start = (bf16[768,512]{0,1:T(8,128)(2,1)}, bf16[768,512]{0,1:T(8,128)(2,1)}, u32[]{:S(2)}, u32[]{:S(2)}) collective-permute-start(bf16[768,512]{0,1:T(8,128)(2,1)} %bitcast.5), channel_id=1, source_target_pairs={{0,16},{16,32},{32,48},{48,64},{64,80},{80,96},{96,112},{112,128},... | collective-permute-start | bytes 2359304 | tf_op jit(solution)/shard_map/ppermute | solution.py:29
  363.7 7.8 %copy-start.1 = (pred[768,2304]{0,1:T(8,128)(4,1)S(1)}, pred[768,2304]{0,1:T(8,128)(4,1)}, u32[]{:S(2)}) copy-start(pred[768,2304]{0,1:T(8,128)(4,1)} %compare_and_fusion) | copy-start | bytes 5308420
  371.6 4.2 copy-start.3
  379.8 6.9 %copy-start.5 = (bf16[768,2,1,128]{0,3,2,1:T(8,128)(2,1)S(1)}, bf16[768,2,1,128]{0,3,2,1:T(8,128)(2,1)}, u32[]{:S(2)}) copy-start(bf16[768,2,1,128]{0,3,2,1:T(8,128)(2,1)} %get-tuple-element.297) | copy-start | bytes 1179652
  379.9 7.8 %copy-start.4 = (bf16[768,2,1,128]{0,3,2,1:T(8,128)(2,1)S(1)}, bf16[768,2,1,128]{0,3,2,1:T(8,128)(2,1)}, u32[]{:S(2)}) copy-start(bf16[768,2,1,128]{0,3,2,1:T(8,128)(2,1)} %get-tuple-element.295) | copy-start | bytes 1179652
Sparse Core Ops, SparseCore 0:
  11.3 93.3 all-gather.9
  107.5 122.0 all-gather.7
  231.4 74.3 all-gather.5
  307.3 71.9 all-gather.13
  385.7 75.8 all-gather.11
